TPU v7x, 128 devices: a whole 4x4x4 slice. The times are simulated.
128 devices in a mesh: tokens: 8 (over x_lo, y), tensor: 16 (over z, x_hi, core).
Axes of the slice: x: 4 (x_hi: 2, x_lo: 2; x = x_hi * 2 + x_lo), y: 4, z: 4, core: 2. Of those that a mesh axis runs over, the one named last changes fastest.
Arguments:
- codes: int32 [2, 6144, 5120], P(None, ('tokens', 'tensor')), may hold values from 0 to 254, as said below
- scales: int32 [2, 6144, 160], P(None, ('tokens', 'tensor')), may hold values from 119 to 122
- w_qkv: bfloat16 [5120, 15360], P(None, 'tensor'), may hold values from -0.078125 to 0.078125
- w_rate: bfloat16 [5120, 48], replicated, may hold values from -0.078125 to 0.078125
- rate_bias: float32 [48], P('tensor'), may hold values from -4 to 1
- fast_gate: float32 [16, 320, 320], P('tensor'), may hold values from -0.3125 to 0.3125
- fast_lift: float32 [16, 320, 320], P('tensor'), may hold values from -0.3125 to 0.3125
- fast_down: float32 [16, 320, 320], P('tensor'), may hold values from -0.3125 to 0.3125
- out_gain: float32 [5120], P('tensor'), may hold values from 0.5 to 1.5
Outputs:
- outputs: bfloat16 [2, 6144, 5120], P(None, 'tokens', 'tensor')
Inputs may be any that keep to these rules, and one draw needn't show every extreme that they name: E4M3 codes: bit 7 is the sign, bits 3 to 6 the exponent, bits 0 to 2 the mantissa; 127 and 255 never occur.
All inputs are finite; a program needn't handle non-finite values.
Results may differ from a plain program's by a relative error of at most 0.039.
Values may be sent and summed in bfloat16 or wider, within the bound.
A program may use at most 128 MiB of HBM per device.

v0:
```python
import math

import jax
import jax.numpy as jnp
from jax import lax
from jax.sharding import PartitionSpec as P

epsilon = 1e-06
rate_base = 0.15


def dequantize(codes, scales):
    negative = jnp.where(codes >= 128, -1, 1).astype(jnp.int32)
    lower = codes % 128
    exponent = lower // 8
    mantissa = lower % 8
    significand = jnp.where(exponent == 0, mantissa, mantissa + 8) * negative
    shift_part = jnp.maximum(exponent, 1) - 1
    shape = codes.shape
    grouped = significand.reshape(shape[:-1] + (shape[-1] // 32, 32))
    shifts = shift_part.reshape(shape[:-1] + (shape[-1] // 32, 32)) + (scales - 119)[..., None]
    whole = grouped * jnp.left_shift(jnp.ones_like(shifts), shifts)
    values = whole.astype(jnp.float32) * (1.0 / 131072.0)
    return values.reshape(shape).astype(jnp.bfloat16)


def rms_norm(field):
    return field * lax.rsqrt(jnp.mean(field * field, axis=-1, keepdims=True) + epsilon)


def renorm(old, delta):
    summed = old + delta
    old_scale = jnp.sqrt(jnp.mean(old * old, axis=-1, keepdims=True) + epsilon)
    return (
        summed * old_scale * lax.rsqrt(jnp.mean(summed * summed, axis=-1, keepdims=True) + epsilon)
    )


def local(codes, scales, w_qkv, w_rate, rate_bias, fast_gate, fast_lift, fast_down, out_gain):
    local_rows = dequantize(codes, scales)
    rate_logits = jnp.dot(local_rows, w_rate, preferred_element_type=jnp.float32)
    rates_all = lax.all_to_all(rate_logits, "tensor", split_axis=2, concat_axis=1, tiled=True)
    blocks = local_rows.shape[0]
    heads_dev = fast_gate.shape[0]
    head_size = fast_gate.shape[1]
    tok_count = rates_all.shape[1]
    factor = rate_base / math.sqrt(tok_count * lax.axis_size("tokens"))
    bias_local = rate_bias.reshape(heads_dev, 3)
    gain_local = out_gain.reshape(heads_dev, head_size)
    gate_w, lift_w, down_w = (fast_gate, fast_lift, fast_down)
    results = []
    for block in range(blocks):
        projected = jnp.dot(
            lax.all_gather(local_rows[block], "tensor", axis=0, tiled=True),
            w_qkv,
            preferred_element_type=jnp.float32,
        ).astype(jnp.bfloat16)
        projected = projected.reshape(tok_count, heads_dev, 3, head_size)
        queries = projected[:, :, 0]
        key_rows = projected[:, :, 1]
        value_rows = projected[:, :, 2]
        query_norm = rms_norm(queries.astype(jnp.float32)).astype(jnp.bfloat16)
        key_norm = rms_norm(key_rows.astype(jnp.float32)).astype(jnp.bfloat16)
        rates_now = (
            jax.nn.softplus(rates_all[block].reshape(tok_count, heads_dev, 3) + bias_local) * factor
        )
        gate_b = gate_w.astype(jnp.bfloat16)
        lift_b = lift_w.astype(jnp.bfloat16)
        down_b = down_w.astype(jnp.bfloat16)
        gate_pre = jnp.einsum("thd,hdf->thf", key_norm, gate_b, preferred_element_type=jnp.float32)
        lift_pre = jnp.einsum("thd,hdf->thf", key_norm, lift_b, preferred_element_type=jnp.float32)
        gate_sig = jax.nn.sigmoid(gate_pre)
        activated = gate_pre * gate_sig
        hidden = (activated * lift_pre).astype(jnp.bfloat16)
        hidden_grad = jnp.einsum(
            "thd,hfd->thf", value_rows, down_b, preferred_element_type=jnp.float32
        )
        gate_grad = (
            hidden_grad * lift_pre * gate_sig * (1.0 + gate_pre * (1.0 - gate_sig))
        ).astype(jnp.bfloat16)
        lift_grad = (hidden_grad * activated).astype(jnp.bfloat16)
        key_gate = (key_norm.astype(jnp.float32) * rates_now[:, :, 0:1]).astype(jnp.bfloat16)
        key_lift = (key_norm.astype(jnp.float32) * rates_now[:, :, 1:2]).astype(jnp.bfloat16)
        hidden_rate = (hidden.astype(jnp.float32) * rates_now[:, :, 2:3]).astype(jnp.bfloat16)
        delta_gate = jnp.einsum(
            "thd,thf->hdf", key_gate, gate_grad, preferred_element_type=jnp.float32
        )
        delta_lift = jnp.einsum(
            "thd,thf->hdf", key_lift, lift_grad, preferred_element_type=jnp.float32
        )
        delta_down = jnp.einsum(
            "thf,thd->hfd", hidden_rate, value_rows, preferred_element_type=jnp.float32
        )
        summed = (
            lax.psum(delta_gate.astype(jnp.bfloat16), "tokens").astype(jnp.float32),
            lax.psum(delta_lift.astype(jnp.bfloat16), "tokens").astype(jnp.float32),
            lax.psum(delta_down.astype(jnp.bfloat16), "tokens").astype(jnp.float32),
        )
        gate_w = renorm(gate_w, summed[0])
        lift_w = renorm(lift_w, summed[1])
        down_w = renorm(down_w, summed[2])
        query_gate = jnp.einsum(
            "thd,hdf->thf",
            query_norm,
            gate_w.astype(jnp.bfloat16),
            preferred_element_type=jnp.float32,
        )
        query_lift = jnp.einsum(
            "thd,hdf->thf",
            query_norm,
            lift_w.astype(jnp.bfloat16),
            preferred_element_type=jnp.float32,
        )
        query_hidden = (jax.nn.silu(query_gate) * query_lift).astype(jnp.bfloat16)
        fast_out = jnp.einsum(
            "thf,hfd->thd",
            query_hidden,
            down_w.astype(jnp.bfloat16),
            preferred_element_type=jnp.float32,
        )
        normed = (rms_norm(fast_out) * gain_local).astype(jnp.bfloat16)
        results.append(normed.reshape(tok_count, heads_dev * head_size))
    return jnp.stack(results, 0)


def solution(mesh):
    return jax.shard_map(
        local,
        mesh=mesh,
        in_specs=(
            P(None, ("tokens", "tensor"), None),
            P(None, ("tokens", "tensor"), None),
            P(None, "tensor"),
            P(),
            P("tensor"),
            P("tensor", None, None),
            P("tensor", None, None),
            P("tensor", None, None),
            P("tensor"),
        ),
        out_specs=P(None, "tokens", "tensor"),
        check_vma=False,
    )
```

profile of v0, /device:TPU:0, one launch (start us, length us, event | category | flops | bytes accessed | tf_op | source)
XLA Modules:
  0.0 366.2 jit_solution(10892156515383249694)
XLA Ops:
  6.5 0.0 all-gather.7.cloned.1.call-start
  6.5 1.0 broadcast_add_fusion
  7.5 6.3 %add.277 = s32[2,48,160,32]{3,2,1,0:T(8,128)} broadcast(s32[2,48,160]{2,1,0:T(8,128)S(1)} %broadcast_add_fusion), dimensions={0,1,2} | broadcast | bytes 2027520 | tf_op jit(solution)/shard_map/add | solution.py:21
  13.8 5.9 %add.278 = s32[2,48,5120]{2,1,0:T(8,128)S(1)} reshape(s32[2,48,160,32]{3,2,1,0:T(8,128)} %add.277) | data formatting | bytes 3932160 | tf_op jit(solution)/shard_map/add | solution.py:21
  19.8 4.5 %fusion.9 = bf16[2,48,5120]{2,1,0:T(8,128)(2,1)S(1)} fusion(s32[2,48,5120]{2,1,0:T(8,128)S(1)} %add.278, s32[2,48,5120]{2,1,0:T(8,128)} %param.9), kind=kLoop, calls=%fused_computation.18 | loop fusion | flops 21626880 | bytes 4915200 | tf_op jit(solution)/shard_map/convert_element_type | solution.py:24
  24.3 1.0 fusion.143
  25.3 0.0 all-gather.7.cloned.1.call-update
  25.3 0.0 all-gather.5.cloned.1.call-start
  25.4 0.7 all-gather.5.cloned.1.call-update
  26.1 0.0 all-reduce.7.cloned.1.call-start
  26.1 0.4 fusion.68
  26.5 0.1 copy.13
  26.6 0.1 reshape.730
  26.8 15.4 %all_to_all.15 = f32[16,1,288]{2,1,0:T(1,128)S(1)} all-to-all(f32[16,1,288]{2,1,0:T(1,128)S(1)} %reshape.730), channel_id=1, replica_groups=mesh['tokens'=8,'tensor'=16] {'tensor'}, dimensions={0} | all-to-all | bytes 36864 | tf_op jit(solution)/shard_map/all_to_all | solution.py:42
  42.1 0.5 broadcast.489
  42.6 0.7 reduce.36
  43.3 0.1 reshape.731
  43.5 0.1 reshape_squeeze.6
  43.6 0.1 reshape_squeeze.7
  43.7 0.2 fusion.133
  43.9 54.9 %all-gather.7.cloned.1.call-done = bf16[1,768,5120]{2,1,0:T(8,128)(2,1)} async-done(((bf16[1,48,5120]{2,1,0:T(8,128)(2,1)}), bf16[1,768,5120]{2,1,0:T(8,128)(2,1)}) %all-gather.7.cloned.1.call-update) | async-done | bytes 7864336 | tf_op jit(solution)/shard_map/all_gather | solution.py:54
  98.9 12.8 %fusion.15 = bf16[768,960]{0,1:T(8,128)(2,1)S(1)} fusion(bf16[5120,960]{0,1:T(8,128)(2,1)} %param.11, bf16[1,768,5120]{2,1,0:T(8,128)(2,1)} %all-gather.7.cloned.1.call-done), kind=kOutput, calls=%fused_computation.23 | convolution fusion | flops 7550484480 | bytes 19169280 | tf_op jit(solution)/shard_map/dot_general | solution.py:53
  111.6 0.2 fusion.36
  111.8 0.0 copy-start.1
  111.9 58.1 %all-gather.5.cloned.1.call-done = bf16[1,768,5120]{2,1,0:T(8,128)(2,1)} async-done(((bf16[1,48,5120]{2,1,0:T(8,128)(2,1)}), bf16[1,768,5120]{2,1,0:T(8,128)(2,1)}) %all-gather.5.cloned.1.call-update) | async-done | bytes 7864336 | tf_op jit(solution)/shard_map/all_gather | solution.py:54
  170.0 12.8 %fusion.12 = bf16[768,960]{0,1:T(8,128)(2,1)S(1)} fusion(bf16[5120,960]{0,1:T(8,128)(2,1)} %param.11, bf16[1,768,5120]{2,1,0:T(8,128)(2,1)} %all-gather.5.cloned.1.call-done), kind=kOutput, calls=%fused_computation.22 | convolution fusion | flops 7550484480 | bytes 19169280 | tf_op jit(solution)/shard_map/dot_general | solution.py:53
  182.8 0.0 copy-start.3
  182.8 0.2 fusion.34
  183.0 0.0 copy-start.2
  183.0 0.5 convolution_bitcast_fusion.11
  183.5 0.7 copy-done.3
  184.2 0.5 convolution_bitcast_fusion.10
  184.6 0.4 convolution_bitcast_fusion
  185.1 1.2 fusion.24
  186.2 1.4 fusion.25
  187.6 0.0 copy-done.4
  187.6 1.2 fusion.26
  188.8 0.0 all-reduce.7.cloned.1.call-update
  188.9 0.3 all-reduce.5.cloned.1.call-start
  189.2 73.6 %all-reduce.7.cloned.1.call-done = (bf16[1,320,320]{2,1,0:T(8,128)(2,1)}, bf16[1,320,320]{2,1,0:T(8,128)(2,1)}, bf16[1,320,320]{2,1,0:T(8,128)(2,1)}) async-done(((bf16[1,320,320]{2,1,0:T(8,128)(2,1)}, bf16[1,320,320]{2,1,0:T(8,128)(2,1)}, bf16[1,320,320]{2,1,0:T(8,128)(2,1)}), (bf16[1,320,320]{2,1,0:T(8,128)(2,1)}, bf16[1,320,320]{2,1,0:T(8,128)(2,1)}, ...) | async-done | bytes 614416 | tf_op jit(solution)/shard_map/psum | solution.py:95
  262.8 1.2 multiply_reduce_fusion.11
  264.0 1.1 multiply_reduce_fusion.13
  265.2 1.1 multiply_reduce_fusion.9
  266.4 0.2 fusion.89
  266.6 0.2 fusion.90
  266.8 0.4 convolution_bitcast_fusion.6
  267.2 0.4 convolution_bitcast_fusion.5
  267.7 0.1 copy-done.9
  267.8 0.2 fusion.91
  268.0 0.4 convolution_bitcast_fusion.4
  268.4 0.3 copy-done.12
  268.6 1.2 fusion.27
  269.8 1.4 fusion.28
  271.2 1.2 fusion.29
  272.4 0.0 all-reduce.5.cloned.1.call-update
  272.4 2.6 convolution_bitcast_fusion.9
  275.0 3.4 multiply_reduce_fusion.1
  278.4 69.6 %all-reduce.5.cloned.1.call-done = (bf16[1,320,320]{2,1,0:T(8,128)(2,1)}, bf16[1,320,320]{2,1,0:T(8,128)(2,1)}, bf16[1,320,320]{2,1,0:T(8,128)(2,1)}) async-done(((bf16[1,320,320]{2,1,0:T(8,128)(2,1)}, bf16[1,320,320]{2,1,0:T(8,128)(2,1)}, bf16[1,320,320]{2,1,0:T(8,128)(2,1)}), (bf16[1,320,320]{2,1,0:T(8,128)(2,1)}, bf16[1,320,320]{2,1,0:T(8,128)(2,1)}, ...) | async-done | bytes 614416 | tf_op jit(solution)/shard_map/psum | solution.py:95
  348.1 1.4 multiply_reduce_fusion.7
  349.5 1.9 multiply_reduce_fusion.3
  351.5 1.7 convolution_bitcast_fusion.3
  353.1 3.8 %multiply_reduce_fusion = (f32[768]{0:T(1024)S(1)}, f32[1,320,768]{2,1,0:T(8,128)}) fusion(f32[768,1,320]{0,2,1:T(8,128)} %convolution_bitcast_fusion.3, f32[768]{0:T(1024)S(1)} %add_rsqrt_fusion.1, bf16[768,1,3,320]{0,3,2,1:T(8,128)(2,1)S(1)} %bitcast.240, bf16[1,320,320]{2,1,0:T(8,128)(2,1)} %get-tuple-element.29, f32[320]{0:T(512)S(1)} %add_rsqrt_fusion.6, ...), kind=kOutput, calls=%fused_computation.80 | convolution fusion | flops 319118592 | bytes 4283392 | tf_op jit(solution)/shard_map/thf,hfd->thd/dot_general | solution.py:115
  356.9 1.7 fusion.48
  358.7 1.0 pad_maximum_fusion
  (45 shorter events, 0.3 us)
Async XLA Ops:
  6.5 19.6 %copy-start = (bf16[5120,48]{0,1:T(8,128)(2,1)S(1)}, bf16[5120,48]{0,1:T(8,128)(2,1)}, u32[]{:S(2)}) copy-start(bf16[5120,48]{0,1:T(8,128)(2,1)} %param.12) | copy-start | bytes 1474564
  6.5 92.3 %all-gather.7.cloned.1.call-start = ((), (), s32[]{:S(2)}) async-start(), calls=%async_computation.2 | async-start | bytes 8355840 | tf_op jit(solution)/shard_map/all_gather | solution.py:54
  25.3 18.4 %copy-start.14 = (f32[3]{0:T(128)S(1)}, f32[3]{0:T(128)}, u32[]{:S(2)}) copy-start(f32[3]{0:T(128)} %param.13) | copy-start | bytes 40
  25.3 144.7 %all-gather.5.cloned.1.call-start = ((), (), s32[]{:S(2)}) async-start(), calls=%async_computation.1 | async-start | bytes 8355840 | tf_op jit(solution)/shard_map/all_gather | solution.py:54
  26.1 236.7 %all-reduce.7.cloned.1.call-start = ((), (), s32[]{:S(2)}) async-start(), calls=%async_computation.4 | async-start | bytes 1474560 | tf_op jit(solution)/shard_map/psum | solution.py:95
  111.8 71.2 %copy-start.1 = (f32[1,320,320]{2,1,0:T(8,128)S(1)}, f32[1,320,320]{2,1,0:T(8,128)}, u32[]{:S(2)}) copy-start(f32[1,320,320]{2,1,0:T(8,128)} %param.14) | copy-start | bytes 1228804
  182.8 4.8 %copy-start.4 = (bf16[768,960]{0,1:T(8,128)(2,1)}, bf16[768,960]{0,1:T(8,128)(2,1)S(1)}, u32[]{:S(2)}) copy-start(bf16[768,960]{0,1:T(8,128)(2,1)S(1)} %fusion.12) | copy-start | bytes 4423684
  182.8 1.4 copy-start.3
  183.0 1.6 copy-start.2
  188.9 159.2 %all-reduce.5.cloned.1.call-start = ((), (), s32[]{:S(2)}) async-start(), calls=%async_computation.3 | async-start | bytes 1474560 | tf_op jit(solution)/shard_map/psum | solution.py:95
  262.8 3.6 copy-start.7
  262.8 3.8 %copy-start.5 = (bf16[1,320,320]{2,1,0:T(8,128)(2,1)S(1)}, bf16[1,320,320]{2,1,0:T(8,128)(2,1)}, u32[]{:S(2)}) copy-start(bf16[1,320,320]{2,1,0:T(8,128)(2,1)} %get-tuple-element.30) | copy-start | bytes 614404
  266.6 1.1 copy-start.11
  266.7 1.2 copy-start.8
  266.7 1.0 copy-start.9
  268.0 0.7 copy-start.12
  348.1 3.4 copy-start.6
  348.1 3.4 copy-start.10
  353.1 3.8 %copy-start.13 = (f32[320]{0:T(512)S(1)}, f32[320]{0:T(512)}, u32[]{:S(2)}) copy-start(f32[320]{0:T(512)} %param.17) | copy-start | bytes 3844
Sparse Core Ops, SparseCore 0:
  25.4 73.3 all-gather.6
  101.3 68.6 all-gather.4
  189.0 73.7 all-reduce.6
  272.6 75.4 all-reduce.4
where the time goes:
time: 367 us; the launch traced here: 366 us
  waiting for transfers between devices  257 us (70%)
  matrix products  47.6 us (13%)
  other arithmetic  16.9 us (5%)
  local copies, waits for them, and re-layouts  15.5 us (4%)
  blocking collectives  15.4 us (4%)
  between operations  13.6 us (4%)
    psum x2, waiting for transfers between devices, local(): lax.psum(delta_gate.astype(jnp.bfloat16), 'tokens').astype(jnp.float32)  143 us
    all_gather x2, waiting for transfers between devices, local(): lax.all_gather(local_rows[block], 'tensor', axis=0, tiled=True)  113 us
    dot_general x2, matrix products, local(): jnp.dot(lax.all_gather(local_rows[block], 'tensor', axis=0, tiled=True),...  25.5 us
    all_to_all x1, blocking collectives, local(): lax.all_to_all(rate_logits, 'tensor', split_axis=2, concat_axis=1, tiled=...  15.4 us
    add x2, local copies, waits for them, and re-layouts, dequantize(): shift_part.reshape(shape[:-1] + (shape[-1] // 32, 32))  12.3 us
  transfers between devices with their start and end apart: 4, of which 4 were waited for; matrix products, arithmetic and copies ran while one was open for 6% of the time, Pallas kernels for 0%

commit v1 on v0

v1 whole, which is shorter than its diff:
```python
import functools
import math

import jax
import jax.numpy as jnp
from jax import lax
from jax.experimental import pallas as pl
from jax.experimental.pallas import tpu as pltpu
from jax.sharding import PartitionSpec as P

epsilon = 1e-06
rate_base = 0.15

MESH = pl.DeviceIdType.MESH
BF = jnp.bfloat16
F32 = jnp.float32

UNIT = 16
HALVES = 2
AHEAD = 1
LAG = 2
KEYS = 384
PAD = 64


def dot(a, b):
    return jnp.dot(a, b, preferred_element_type=F32)


def dot_tn(a, b):
    return lax.dot_general(a, b, (((0,), (0,)), ((), ())), preferred_element_type=F32)


def dot_nt(a, b):
    return lax.dot_general(a, b, (((1,), (1,)), ((), ())), preferred_element_type=F32)


def kernel(
    factor,
    codes_hbm,
    scales_ref,
    wqkv_hbm,
    wrate_hbm,
    bias_ref,
    gate_ref,
    lift_ref,
    down_ref,
    gain_ref,
    out_ref,
    acts,
    w,
    w_rate,
    w_last,
    codes,
    spread,
    factors,
    acc,
    stack,
    master,
    rs_send,
    rs_recv,
    fast,
    queries,
    keys,
    values,
    rates,
    local_sem,
    send_sem,
    z_sem,
    x_sem,
    part_a_sem,
    part_b_sem,
    near_sem,
    far_sem,
    rs_send_sem,
    rs_sem,
    ag_send_sem,
    ag_sem,
):
    rounds, sources, unit, width = acts.shape
    units = rounds // HALVES
    part_a = width * 2 // 5 // 128 * 128
    depth = w.shape[0]
    head = gate_ref.shape[1]
    tokens = sources * unit
    t = lax.axis_index("tokens")
    h = lax.axis_index("tensor")
    shards = 8
    z, hi, core = h // 4, (h // 2) % 2, h % 2

    def at(dz, other):
        side = 1 - hi if other else hi
        return lax.rem(z + dz, 4) * 4 + side * 2 + core

    z_peers = [at(dz, False) for dz in (1, 3, 2)]
    x_peer = at(0, True)
    diagonal = [at(dz, True) for dz in (1, 3, 2)]
    sibling = h + 1 - 2 * core
    t_peers = [lax.rem(t + k, shards) for k in range(1, shards)]

    barrier = pltpu.get_barrier_semaphore()
    for peer in z_peers + [x_peer, sibling]:
        pl.semaphore_signal(barrier, inc=1, device_id=(t, peer), device_id_type=MESH)
    for peer in t_peers:
        pl.semaphore_signal(barrier, inc=1, device_id=(peer, h), device_id_type=MESH)

    codes_copy = pltpu.make_async_copy(codes_hbm, codes, local_sem.at[0])
    w_copy = pltpu.make_async_copy(wqkv_hbm, w, local_sem.at[1])
    rate_copy = pltpu.make_async_copy(wrate_hbm, w_rate, local_sem.at[2])
    codes_copy.start()
    w_copy.start()
    rate_copy.start()

    groups = scales_ref.shape[1]
    group = lax.broadcasted_iota(jnp.int32, (groups, depth), 0)
    column = lax.broadcasted_iota(jnp.int32, (groups, depth), 1)
    spread[...] = jnp.where(
        lax.shift_right_logical(column, 5) == group, 1.0, 0.0
    ).astype(BF)
    powers = lax.shift_left(jnp.ones_like(scales_ref[...]), scales_ref[...] - 119)
    powers = powers.astype(F32).astype(BF)
    step_n = 512

    def spread_step(n, carry):
        cols = pl.ds(pl.multiple_of(n * step_n, step_n), step_n)
        factors[:, cols] = dot(powers, spread[:, cols]) * (1.0 / 131072.0)
        return carry

    lax.fori_loop(0, depth // step_n, spread_step, 0)
    codes_copy.wait()

    def decode(r, carry):
        rows = pl.ds(pl.multiple_of((r // HALVES) * unit, unit), unit)
        for n in range(width // step_n):
            start = (r % HALVES) * width + n * step_n
            cols = pl.ds(pl.multiple_of(start, step_n), step_n)
            code = codes[rows, cols]
            lower = jnp.bitwise_and(code, 127)
            exponent = lax.shift_right_logical(lower, 3)
            mantissa = jnp.bitwise_and(lower, 7)
            normal = exponent > 0
            significand = jnp.where(normal, mantissa + 8, mantissa)
            significand = jnp.where(code >= 128, -significand, significand)
            shift = jnp.where(normal, exponent - 1, 0)
            whole = lax.shift_left(significand, shift).astype(F32)
            acts[r, h, :, n * step_n : (n + 1) * step_n] = (
                whole * factors[rows, cols]
            ).astype(BF)
        return carry

    def remote(src, dst, send, recv, tok, ten):
        pltpu.make_async_remote_copy(
            src_ref=src,
            dst_ref=dst,
            send_sem=send,
            recv_sem=recv,
            device_id=(tok, ten),
            device_id_type=MESH,
        ).start()

    def wait(ref, sem):
        pltpu.make_async_copy(ref, ref, sem).wait()

    def send_own(s):
        mine = acts.at[s, h]
        for peer in z_peers:
            remote(mine, mine, send_sem.at[s], z_sem.at[s], t, peer)
        remote(mine, mine, send_sem.at[s], x_sem.at[s], t, x_peer)
        remote(mine, mine, send_sem.at[s], near_sem.at[s], t, sibling)

    def forward(s):
        wait(acts.at[s, 0:3], z_sem.at[s])
        for peer in z_peers:
            part = acts.at[s, peer, :, part_a:width]
            remote(part, part, send_sem.at[s], part_b_sem.at[s], t, x_peer)
        for peer in z_peers:
            item = acts.at[s, peer]
            remote(item, item, send_sem.at[s], near_sem.at[s], t, sibling)
        wait(acts.at[s, 0], x_sem.at[s])
        part = acts.at[s, x_peer, :, 0:part_a]
        for peer in z_peers:
            remote(part, part, send_sem.at[s], part_a_sem.at[s], t, peer)
        item = acts.at[s, x_peer]
        remote(item, item, send_sem.at[s], near_sem.at[s], t, sibling)

    def forward_far(s):
        wait(acts.at[s, 0:3, :, 0:part_a], part_a_sem.at[s])
        wait(acts.at[s, 0:3, :, part_a:width], part_b_sem.at[s])
        for peer in diagonal:
            item = acts.at[s, peer]
            remote(item, item, send_sem.at[s], far_sem.at[s], t, sibling)

    decode(0, 0)
    pl.semaphore_wait(barrier, 12)
    for s in range(AHEAD):
        if s > 0:
            decode(s, 0)
        send_own(s)
    lax.fori_loop(AHEAD, rounds, decode, 0)

    stack[...] = jnp.zeros_like(stack)
    stack[PAD : PAD + head, 0:head] = gate_ref[0]
    stack[PAD + head : PAD + 2 * head, 0:head] = lift_ref[0]
    stack[PAD + 2 * head : PAD + 3 * head, 0:head] = down_ref[0]
    fast[0] = stack[...].astype(BF)
    shard = stack.shape[0] // shards
    own_rows = pl.ds(pl.multiple_of(t * shard, shard), shard)
    master[...] = stack[own_rows, :]
    stack[...] = jnp.zeros_like(stack)

    w_copy.wait()
    rate_copy.wait()
    main = 3 * head // 256 * 256
    tail = 3 * head - main
    rate_cols = w_rate.shape[1]

    def last_step(n, carry):
        rows = pl.ds(pl.multiple_of(n * 512, 512), 512)
        w_last[rows, :] = jnp.concatenate(
            [
                w[rows, main : 3 * head],
                w_rate[rows, :],
                jnp.zeros((512, 256 - tail - rate_cols), BF),
            ],
            axis=1,
        )
        return carry

    lax.fori_loop(0, depth // 512, last_step, 0)

    def project(c, half):
        chunk = 512

        def one(k, carry):
            cols = pl.ds(pl.multiple_of(k * chunk, chunk), chunk)
            rows = pl.ds(pl.multiple_of(half * width + k * chunk, chunk), chunk)
            x = acts[c, :, :, cols].reshape(tokens, chunk)
            acc[:, 0:main] += dot(x, w[rows, 0:main])
            acc[:, main : main + 256] += dot(x, w_last[rows, :])
            return carry

        @pl.when(half == 0)
        def _():
            acc[...] = jnp.zeros_like(acc)

        lax.fori_loop(0, width // chunk, one, 0)

    def finish(u):
        q = acc[:, 0:head]
        q = q * lax.rsqrt(jnp.sum(q * q, axis=1, keepdims=True) * (1.0 / head) + epsilon)
        queries[u] = q.astype(BF)
        k = acc[:, head - PAD : 2 * head]
        lane = lax.broadcasted_iota(jnp.int32, k.shape, 1)
        k = jnp.where(lane >= PAD, k, 0.0)
        k = k * lax.rsqrt(jnp.sum(k * k, axis=1, keepdims=True) * (1.0 / head) + epsilon)
        keys[u] = k.astype(BF)
        values[u] = acc[:, 2 * head : 3 * head].astype(BF)
        logits = acc[:, main + 128 : main + 256]
        lane = lax.broadcasted_iota(jnp.int32, logits.shape, 1)
        first = tail - 128 + 3 * h
        picked = jnp.zeros(logits.shape, F32)
        for i in range(3):
            mine = jnp.where(lane == first + i, logits, 0.0)
            column = jnp.sum(mine, axis=1, keepdims=True) + bias_ref[0, i]
            picked = jnp.where(lane == i, column, picked)
        soft = jnp.maximum(picked, 0.0) + jnp.log1p(jnp.exp(-jnp.abs(picked)))
        rates[u] = soft * factor

    def key_step(u, carry):
        version = u // (units // 2)
        kn = keys[u]
        v = values[u]
        rate = rates[u]
        gate_pre = dot(kn, fast[version, 0:KEYS, 0:head])
        lift_pre = dot(kn, fast[version, head : head + KEYS, 0:head])
        hidden_grad = dot_nt(v, fast[version, PAD + 2 * head : PAD + 3 * head, 0:head])
        sig = jax.nn.sigmoid(gate_pre)
        activated = gate_pre * sig
        hidden = activated * lift_pre
        gate_grad = hidden_grad * lift_pre * (sig * (1.0 + gate_pre * (1.0 - sig)))
        lift_grad = hidden_grad * activated
        gate_grad = (gate_grad * rate[:, 0:1]).astype(BF)
        lift_grad = (lift_grad * rate[:, 1:2]).astype(BF)
        hidden = (hidden * rate[:, 2:3]).astype(BF)
        stack[0:KEYS, 0:head] += dot_tn(kn, gate_grad)
        stack[KEYS : KEYS + head, 0:head] += dot_tn(kn, lift_grad)[PAD:KEYS]
        stack[KEYS + head : KEYS + 2 * head, 0:head] += dot_tn(hidden, v)
        return carry

    def reduce_send(block):
        rs_send[...] = stack[...].astype(BF)
        stack[...] = jnp.zeros_like(stack)
        for peer in t_peers:
            rows = pl.ds(pl.multiple_of(peer * shard, shard), shard)
            remote(
                rs_send.at[rows],
                rs_recv.at[block, t],
                rs_send_sem.at[block],
                rs_sem.at[block],
                peer,
                h,
            )
        rs_recv[block, t] = rs_send[own_rows, :]

    def reduce_finish(block):
        wait(rs_recv.at[block, 0:7], rs_sem.at[block])
        wait(rs_send.at[0 : 7 * shard], rs_send_sem.at[block])
        summed = rs_recv[block, 0].astype(F32)
        for j in range(1, shards):
            summed = summed + rs_recv[block, j].astype(F32)
        old = master[...]
        summed = old + summed
        old_scale = jnp.sqrt(
            jnp.sum(old * old, axis=1, keepdims=True) * (1.0 / head) + epsilon
        )
        new_scale = lax.rsqrt(
            jnp.sum(summed * summed, axis=1, keepdims=True) * (1.0 / head) + epsilon
        )
        new = summed * old_scale * new_scale
        master[...] = new
        fast[block + 1, own_rows, :] = new.astype(BF)
        mine = fast.at[block + 1, own_rows]
        for peer in t_peers:
            remote(mine, mine, ag_send_sem.at[block], ag_sem.at[block], peer, h)

    def gather_finish(block):
        wait(fast.at[block + 1, 0 : 7 * shard], ag_sem.at[block])
        wait(fast.at[block + 1, 0 : 7 * shard], ag_send_sem.at[block])

    def query_step(u, carry):
        block = u // (units // 2)
        q = queries[u]
        gate_pre = dot(q, fast[block + 1, PAD : PAD + head, 0:head])
        lift_pre = dot(q, fast[block + 1, PAD + head : PAD + 2 * head, 0:head])
        hidden = (gate_pre * jax.nn.sigmoid(gate_pre) * lift_pre).astype(BF)
        out = dot(hidden, fast[block + 1, PAD + 2 * head : PAD + 3 * head, 0:head])
        out = out * lax.rsqrt(
            jnp.sum(out * out, axis=1, keepdims=True) * (1.0 / head) + epsilon
        )
        out = (out * gain_ref[...]).astype(BF)
        out_ref[block, :, u % (units // 2)] = out.reshape(sources, unit, head)
        return carry

    per_block = rounds // 2

    def step(s, carry):
        @pl.when(s + AHEAD < rounds)
        def _():
            send_own(s + AHEAD)

        @pl.when(s < rounds)
        def _():
            forward(s)

        @pl.when((s >= 1) & (s < rounds + 1))
        def _():
            forward_far(s - 1)

        c = s - LAG

        @pl.when(c >= 0)
        def _():
            wait(acts.at[c, 0:5], near_sem.at[c])
            wait(acts.at[c, 0:3], far_sem.at[c])
            half = c % HALVES
            u = c // HALVES
            project(c, half)

            @pl.when(half == HALVES - 1)
            def _():
                finish(u)

            @pl.when(c == per_block + 1)
            def _():
                reduce_finish(0)

            @pl.when(c == per_block + 3)
            def _():
                gather_finish(0)

            first = jnp.where(c == per_block + 3, units // 2, u)
            ready = (half == HALVES - 1) & (c != per_block + 1)
            lax.fori_loop(first, jnp.where(ready, u + 1, first), key_step, 0)

            @pl.when(c == per_block - 1)
            def _():
                reduce_send(0)

        return carry

    lax.fori_loop(0, rounds + LAG, step, 0)
    reduce_send(1)
    lax.fori_loop(0, units // 2, query_step, 0)

    def drain(s, carry):
        wait(acts.at[s, 0:15], send_sem.at[s])
        return carry

    lax.fori_loop(0, rounds, drain, 0)
    reduce_finish(1)
    gather_finish(1)
    lax.fori_loop(units // 2, units, query_step, 0)


def local(codes, scales, w_qkv, w_rate, rate_bias, fast_gate, fast_lift, fast_down, out_gain):
    blocks, rows, depth = codes.shape
    head = fast_gate.shape[1]
    sources = lax.axis_size("tensor")
    shards = lax.axis_size("tokens")
    units = blocks * rows // UNIT
    rounds = units * HALVES
    tokens = sources * UNIT
    width = depth // HALVES
    factor = rate_base / math.sqrt(rows * sources * shards)
    stacked = 3 * head + PAD
    vmem = pl.BlockSpec(memory_space=pltpu.VMEM)
    smem = pl.BlockSpec(memory_space=pltpu.SMEM)
    anyspace = pl.BlockSpec(memory_space=pl.ANY)
    dma = pltpu.SemaphoreType.DMA
    out = pl.pallas_call(
        functools.partial(kernel, factor),
        out_shape=jax.ShapeDtypeStruct((blocks, sources, rows // UNIT, UNIT, head), BF),
        in_specs=[anyspace, vmem, anyspace, anyspace, smem, vmem, vmem, vmem, vmem],
        out_specs=vmem,
        scratch_shapes=[
            pltpu.VMEM((rounds, sources, UNIT, width), BF),
            pltpu.VMEM((depth, 3 * head), BF),
            pltpu.VMEM((depth, w_rate.shape[1]), BF),
            pltpu.VMEM((depth, 256), BF),
            pltpu.VMEM((blocks * rows, depth), jnp.int32),
            pltpu.VMEM((scales.shape[2], depth), BF),
            pltpu.VMEM((blocks * rows, depth), F32),
            pltpu.VMEM((tokens, 1024), F32),
            pltpu.VMEM((stacked, KEYS), F32),
            pltpu.VMEM((stacked // shards, KEYS), F32),
            pltpu.VMEM((stacked, KEYS), BF),
            pltpu.VMEM((2, shards, stacked // shards, KEYS), BF),
            pltpu.VMEM((3, stacked, KEYS), BF),
            pltpu.VMEM((units, tokens, head), BF),
            pltpu.VMEM((units, tokens, KEYS), BF),
            pltpu.VMEM((units, tokens, head), BF),
            pltpu.VMEM((units, tokens, 128), F32),
            dma((3,)),
            dma((rounds,)),
            dma((rounds,)),
            dma((rounds,)),
            dma((rounds,)),
            dma((rounds,)),
            dma((rounds,)),
            dma((rounds,)),
            dma((2,)),
            dma((2,)),
            dma((2,)),
            dma((2,)),
        ],
        compiler_params=pltpu.CompilerParams(
            collective_id=0, has_side_effects=True, vmem_limit_bytes=58 << 20
        ),
        name="fast_weights",
    )(
        codes.reshape(blocks * rows, depth),
        scales.reshape(blocks * rows, scales.shape[2]),
        w_qkv,
        w_rate,
        rate_bias.reshape(1, 3),
        fast_gate,
        fast_lift,
        fast_down,
        out_gain.reshape(1, head),
    )
    return out.reshape(blocks, sources * rows, head)


def solution(mesh):
    return jax.shard_map(
        local,
        mesh=mesh,
        in_specs=(
            P(None, ("tokens", "tensor"), None),
            P(None, ("tokens", "tensor"), None),
            P(None, "tensor"),
            P(),
            P("tensor"),
            P("tensor", None, None),
            P("tensor", None, None),
            P("tensor", None, None),
            P("tensor"),
        ),
        out_specs=P(None, "tokens", "tensor"),
        check_vma=False,
    )
```

time: 367 us -> 146 us (0.40)
  waiting for transfers between devices: 257 us -> 0 us
  Pallas kernels: 0 us -> 124 us
  matrix products: 47.6 us -> 0 us
  other arithmetic: 16.9 us -> 0 us
  blocking collectives: 15.4 us -> 0 us
  between operations: 13.6 us -> 0.01 us
  local copies, waits for them, and re-layouts: 15.5 us -> 20.1 us
    psum x2 -> x0, waiting for transfers between devices: 143 us -> none  [local(): lax.psum(delta_gate.astype(jnp.bfloat16), 'tokens').astype(jnp.float32)]
    pallas_call x0 -> x1, Pallas kernels: none -> 124 us  [local(): pl.pallas_call(functools.partial(kernel, factor), out_shape=jax.ShapeDtyp...]
    all_gather x2 -> x0, waiting for transfers between devices: 113 us -> none  [local(): lax.all_gather(local_rows[block], 'tensor', axis=0, tiled=True)]
    dot_general x19 -> x0, matrix products: 47.6 us -> none  [the longest x2 25.5 us: local(): jnp.dot(lax.all_gather(local_rows[block], 'tensor', axis=0, tiled=True),...]
    all_to_all x1 -> x0, blocking collectives: 15.4 us -> none  [local(): lax.all_to_all(rate_logits, 'tensor', split_axis=2, concat_axis=1, tiled=...]
    unnamed x32 -> x2, local copies, waits for them, and re-layouts: 1.32 us -> 16.6 us
    add x2 -> x0, local copies, waits for them, and re-layouts: 12.3 us -> none  [dequantize(): shift_part.reshape(shape[:-1] + (shape[-1] // 32, 32))]
    reduce_sum x7 -> x0, other arithmetic: 7.26 us -> none  [the longest x5 6.84 us: renorm(): old_scale = jnp.sqrt(jnp.mean(old * old, axis=-1, keepdims=True) + epsilon)]
  transfers between devices with their start and end apart: 4 -> 0, of which waited for: 4 -> 0; matrix products, arithmetic and copies ran while one was open for 6% -> 0% of each run, Pallas kernels for 0% -> 0%
where the time goes in v1:
time: 146 us; the launch traced here: 145 us
  Pallas kernels  124 us (85%)
  local copies, waits for them, and re-layouts  20.1 us (14%)
    pallas_call x1, Pallas kernels, local(): pl.pallas_call(functools.partial(kernel, factor), out_shape=jax.ShapeDtyp...  124 us
    unnamed x2, local copies, waits for them, and re-layouts  16.6 us

profile of v1, /device:TPU:0, one launch (start us, length us, event | category | flops | bytes accessed | tf_op | source)
XLA Modules:
  0.0 144.6 jit_solution(9225470836214104694)
XLA Ops:
  0.0 1.2 reshape.18.gain_ref
  1.2 2.3 %copy.11.wrate_hbm = bf16[5120,48]{1,0:T(8,128)(2,1)} copy(bf16[5120,48]{0,1:T(8,128)(2,1)} %param.12) | data formatting | bytes 983040 | tf_op args[3]
  3.5 14.3 %copy.10.wqkv_hbm = bf16[5120,960]{1,0:T(8,128)(2,1)} copy(bf16[5120,960]{0,1:T(8,128)(2,1)} %param.11) | data formatting | bytes 19660800 | tf_op args[2]
  17.8 124.5 %fast_weights.1 = bf16[2,16,3,16,320]{4,3,2,1,0:T(8,128)(2,1)} custom-call(s32[96,5120]{1,0:T(8,128)} %bitcast.5, s32[96,160]{1,0:T(8,128)} %bitcast.6, bf16[5120,960]{1,0:T(8,128)(2,1)} %copy.10.wqkv_hbm, bf16[5120,48]{1,0:T(8,128)(2,1)} %copy.11.wrate_hbm, f32[1,3]{1,0:T(1,128)} %bitcast.7, f32[1,320,320]{2,1,0:T(8,128)} %gate_ref.1, ...), custom_call_target="tpu_custom_call" | custom-call | tf_op jit(solution)/shard_map/fast_weights/pallas_call | solution.py:420
  142.3 2.3 %copy.12 = bf16[2,768,320]{1,2,0:T(8,128)(2,1)} copy(bf16[2,768,320]{2,1,0:T(8,128)(2,1)} %bitcast.4) | data formatting | bytes 1966080 | tf_op jit(solution)/shard_map/reshape | solution.py:471

commit v2 on v1

v2 whole, which is shorter than its diff:
```python
import functools
import math

import jax
import jax.numpy as jnp
from jax import lax
from jax.experimental import pallas as pl
from jax.experimental.pallas import tpu as pltpu
from jax.sharding import PartitionSpec as P

epsilon = 1e-06
rate_base = 0.15

MESH = pl.DeviceIdType.MESH
BF = jnp.bfloat16
F32 = jnp.float32

UNIT = 16
HALVES = 2
AHEAD = 1
LAG = 2
KEYS = 384
PAD = 64


def dot(a, b):
    return jnp.dot(a, b, preferred_element_type=F32)


def dot_nt(a, b):
    return lax.dot_general(a, b, (((1,), (1,)), ((), ())), preferred_element_type=F32)


def flip(a):
    return a.astype(F32).T.astype(BF)


def kernel(
    factor,
    codes_hbm,
    scales_ref,
    wqkv_hbm,
    wrate_hbm,
    bias_ref,
    gate_ref,
    lift_ref,
    down_ref,
    gain_ref,
    out_ref,
    acts,
    w,
    codes,
    spread,
    factors,
    kv_acc,
    q_acc,
    stack,
    master,
    rs_send,
    rs_recv,
    fast,
    gate_lift,
    gains,
    queries,
    keys,
    values,
    rates,
    local_sem,
    send_sem,
    z_sem,
    x_sem,
    part_a_sem,
    part_b_sem,
    near_sem,
    far_sem,
    rs_send_sem,
    rs_sem,
    ag_send_sem,
    ag_sem,
):
    blocks, _, sources, rows_dev, width = acts.shape
    per = rows_dev // UNIT
    units = blocks * per
    rounds = units * HALVES
    part_a = width * 2 // 5 // 128 * 128
    depth = w.shape[1]
    head = gate_ref.shape[1]
    tokens = sources * UNIT
    block_tokens = sources * rows_dev
    chunk = 1280
    t = lax.axis_index("tokens")
    h = lax.axis_index("tensor")
    shards = 8
    z, hi, core = h // 4, (h // 2) % 2, h % 2

    def at(dz, other):
        side = 1 - hi if other else hi
        return lax.rem(z + dz, 4) * 4 + side * 2 + core

    z_peers = [at(dz, False) for dz in (1, 3, 2)]
    x_peer = at(0, True)
    diagonal = [at(dz, True) for dz in (1, 3, 2)]
    sibling = h + 1 - 2 * core
    t_peers = [lax.rem(t + k, shards) for k in range(1, shards)]

    barrier = pltpu.get_barrier_semaphore()
    for peer in z_peers + [x_peer, sibling]:
        pl.semaphore_signal(barrier, inc=1, device_id=(t, peer), device_id_type=MESH)
    for peer in t_peers:
        pl.semaphore_signal(barrier, inc=1, device_id=(peer, h), device_id_type=MESH)

    codes_copy = pltpu.make_async_copy(codes_hbm, codes, local_sem.at[0])
    w_copy = pltpu.make_async_copy(wqkv_hbm, w.at[0 : 3 * head], local_sem.at[1])
    rate_copy = pltpu.make_async_copy(
        wrate_hbm, w.at[3 * head : w.shape[0]], local_sem.at[2]
    )
    codes_copy.start()
    w_copy.start()
    rate_copy.start()

    groups = scales_ref.shape[1]
    group = lax.broadcasted_iota(jnp.int32, (groups, depth), 0)
    column = lax.broadcasted_iota(jnp.int32, (groups, depth), 1)
    spread[...] = jnp.where(
        lax.shift_right_logical(column, 5) == group, 1.0, 0.0
    ).astype(BF)
    powers = lax.shift_left(jnp.ones_like(scales_ref[...]), scales_ref[...] - 119)
    powers = powers.astype(F32).astype(BF)
    step_n = 512

    def spread_step(n, carry):
        cols = pl.ds(pl.multiple_of(n * step_n, step_n), step_n)
        factors[:, cols] = dot(powers, spread[:, cols]) * (1.0 / 131072.0)
        return carry

    lax.fori_loop(0, depth // step_n, spread_step, 0)
    codes_copy.wait()

    def place(s):
        u = s // HALVES
        return u // per, s % HALVES, pl.ds(pl.multiple_of((u % per) * UNIT, UNIT), UNIT)

    def item(s, source):
        block, half, rows = place(s)
        return acts.at[block, half, source, rows]

    def decode(s, carry):
        block, half, unit_rows = place(s)
        rows = pl.ds(pl.multiple_of((s // HALVES) * UNIT, UNIT), UNIT)
        for n in range(width // step_n):
            start = half * width + n * step_n
            cols = pl.ds(pl.multiple_of(start, step_n), step_n)
            code = codes[rows, cols]
            lower = jnp.bitwise_and(code, 127)
            exponent = lax.shift_right_logical(lower, 3)
            mantissa = jnp.bitwise_and(lower, 7)
            normal = exponent > 0
            significand = jnp.where(normal, mantissa + 8, mantissa)
            significand = jnp.where(code >= 128, -significand, significand)
            shift = jnp.where(normal, exponent - 1, 0)
            whole = lax.shift_left(significand, shift).astype(F32)
            acts[block, half, h, unit_rows, n * step_n : (n + 1) * step_n] = (
                whole * factors[rows, cols]
            ).astype(BF)
        return carry

    def remote(src, dst, send, recv, tok, ten):
        pltpu.make_async_remote_copy(
            src_ref=src,
            dst_ref=dst,
            send_sem=send,
            recv_sem=recv,
            device_id=(tok, ten),
            device_id_type=MESH,
        ).start()

    def wait(ref, sem):
        pltpu.make_async_copy(ref, ref, sem).wait()

    def several(n, first=0, last=width):
        return acts.at[0, 0, 0:n, 0:UNIT, first:last]

    def send_own(s):
        mine = item(s, h)
        for peer in z_peers:
            remote(mine, mine, send_sem.at[s], z_sem.at[s], t, peer)
        remote(mine, mine, send_sem.at[s], x_sem.at[s], t, x_peer)
        remote(mine, mine, send_sem.at[s], near_sem.at[s], t, sibling)

    def forward(s):
        wait(several(3), z_sem.at[s])
        for peer in z_peers:
            part = item(s, peer).at[:, part_a:width]
            remote(part, part, send_sem.at[s], part_b_sem.at[s], t, x_peer)
        for peer in z_peers:
            whole = item(s, peer)
            remote(whole, whole, send_sem.at[s], near_sem.at[s], t, sibling)
        wait(several(1), x_sem.at[s])
        part = item(s, x_peer).at[:, 0:part_a]
        for peer in z_peers:
            remote(part, part, send_sem.at[s], part_a_sem.at[s], t, peer)
        whole = item(s, x_peer)
        remote(whole, whole, send_sem.at[s], near_sem.at[s], t, sibling)

    def forward_far(s):
        wait(several(3, 0, part_a), part_a_sem.at[s])
        wait(several(3, part_a, width), part_b_sem.at[s])
        for peer in diagonal:
            whole = item(s, peer)
            remote(whole, whole, send_sem.at[s], far_sem.at[s], t, sibling)

    decode(0, 0)
    pl.semaphore_wait(barrier, 12)
    for s in range(AHEAD):
        if s > 0:
            decode(s, 0)
        send_own(s)
    lax.fori_loop(AHEAD, rounds, decode, 0)

    stack[...] = jnp.zeros_like(stack)
    stack[0:head, 0:head] = gate_ref[0]
    stack[head : 2 * head, 0:head] = lift_ref[0]
    stack[2 * head : 3 * head, 0:head] = down_ref[0]
    fast[0] = stack[...].astype(BF)
    shard = stack.shape[0] // shards
    own_rows = pl.ds(pl.multiple_of(t * shard, shard), shard)
    master[...] = stack[own_rows, :]
    stack[...] = jnp.zeros_like(stack)
    gains[...] = jnp.broadcast_to(gain_ref[...][None, :], (128, head)).T

    def turn(version):
        gate_lift[version, 0:head] = flip(fast[version, 0:head, 0:head])
        gate_lift[version, head : 2 * head] = flip(fast[version, head : 2 * head, 0:head])

    turn(0)
    w_copy.wait()
    rate_copy.wait()

    def project_keys(c):
        block, half, rows = place(c)

        def one(k, carry):
            cols = pl.ds(pl.multiple_of(k * chunk, chunk), chunk)
            deep = pl.ds(pl.multiple_of(half * width + k * chunk, chunk), chunk)
            x = acts[block, half, :, rows, cols].reshape(tokens, chunk)
            kv_acc[...] += dot_nt(w[head : w.shape[0], deep], x)
            return carry

        @pl.when(half == 0)
        def _():
            kv_acc[...] = jnp.zeros_like(kv_acc)

        lax.fori_loop(0, width // chunk, one, 0)

    def project_queries(block):
        def one(k, carry):
            half = k // (width // chunk)
            start = (k % (width // chunk)) * chunk
            cols = pl.ds(pl.multiple_of(start, chunk), chunk)
            deep = pl.ds(pl.multiple_of(k * chunk, chunk), chunk)
            x = acts[block, half, :, :, cols].reshape(block_tokens, chunk)
            q_acc[...] += dot_nt(w[0:head, deep], x)
            return carry

        q_acc[...] = jnp.zeros_like(q_acc)
        lax.fori_loop(0, depth // chunk, one, 0)
        for n in range(block_tokens // 256):
            q = q_acc[:, n * 256 : (n + 1) * 256]
            q = q * lax.rsqrt(
                jnp.sum(q * q, axis=0, keepdims=True) * (1.0 / head) + epsilon
            )
            queries[block, n * 256 : (n + 1) * 256] = q.T.astype(BF)

    def finish_keys(u):
        k = kv_acc[0:head]
        k = k * lax.rsqrt(jnp.sum(k * k, axis=0, keepdims=True) * (1.0 / head) + epsilon)
        keys[u] = k.astype(BF)
        values[u] = kv_acc[head : 2 * head].astype(BF)
        for i in range(3):
            logit = kv_acc[pl.ds(2 * head + 3 * h + i, 1), :] + bias_ref[0, i]
            soft = jnp.maximum(logit, 0.0) + jnp.log1p(jnp.exp(-jnp.abs(logit)))
            rates[u, i : i + 1] = soft * factor

    def key_step(u, carry):
        version = u // per
        kn = keys[u]
        v = values[u]
        pre = dot(gate_lift[version], kn)
        gate_pre = pre[0:head]
        lift_pre = pre[head : 2 * head]
        hidden_grad = dot(fast[version, 2 * head : 3 * head, 0:head], v)
        sig = jax.nn.sigmoid(gate_pre)
        activated = gate_pre * sig
        hidden = activated * lift_pre
        gate_grad = hidden_grad * lift_pre * (sig * (1.0 + gate_pre * (1.0 - sig)))
        lift_grad = hidden_grad * activated
        gate_grad = (gate_grad * rates[u, 0:1]).astype(BF)
        lift_grad = (lift_grad * rates[u, 1:2]).astype(BF)
        hidden = (hidden * rates[u, 2:3]).astype(BF)
        stack[0:head, 0:head] += dot_nt(kn, gate_grad)
        stack[head : 2 * head, 0:head] += dot_nt(kn, lift_grad)
        stack[2 * head : 3 * head, 0:head] += dot_nt(hidden, v)
        return carry

    def reduce_send(block):
        rs_send[...] = stack[...].astype(BF)
        for peer in t_peers:
            rows = pl.ds(pl.multiple_of(peer * shard, shard), shard)
            remote(
                rs_send.at[rows],
                rs_recv.at[block, t],
                rs_send_sem.at[block],
                rs_sem.at[block],
                peer,
                h,
            )
        rs_recv[block, t] = rs_send[own_rows, :]
        stack[...] = jnp.zeros_like(stack)

    def reduce_finish(block):
        wait(rs_recv.at[block, 0:7], rs_sem.at[block])
        wait(rs_send.at[0 : 7 * shard], rs_send_sem.at[block])
        summed = rs_recv[block, 0].astype(F32)
        for j in range(1, shards):
            summed = summed + rs_recv[block, j].astype(F32)
        old = master[...]
        summed = old + summed
        old_scale = jnp.sqrt(
            jnp.sum(old * old, axis=1, keepdims=True) * (1.0 / head) + epsilon
        )
        new_scale = lax.rsqrt(
            jnp.sum(summed * summed, axis=1, keepdims=True) * (1.0 / head) + epsilon
        )
        new = summed * old_scale * new_scale
        master[...] = new
        fast[block + 1, own_rows, :] = new.astype(BF)
        mine = fast.at[block + 1, own_rows]
        for peer in t_peers:
            remote(mine, mine, ag_send_sem.at[block], ag_sem.at[block], peer, h)

    def gather_finish(block):
        wait(fast.at[block + 1, 0 : 7 * shard], ag_sem.at[block])

    def query_pass(block):
        version = block + 1
        down = flip(fast[version, 2 * head : 3 * head, 0:head])
        gain = jnp.concatenate([gains[...], gains[...]], axis=1)
        for n in range(block_tokens // 256):
            span = slice(n * 256, (n + 1) * 256)
            q = queries[block, span]
            gate_pre = dot(q, fast[version, 0:head, 0:head])
            lift_pre = dot(q, fast[version, head : 2 * head, 0:head])
            hidden = (gate_pre * jax.nn.sigmoid(gate_pre) * lift_pre).astype(BF)
            out = dot_nt(down, hidden)
            out = out * lax.rsqrt(
                jnp.sum(out * out, axis=0, keepdims=True) * (1.0 / head) + epsilon
            )
            out_ref[block, :, span] = (out * gain).astype(BF)

    per_block = rounds // 2

    def step(s, carry):
        @pl.when(s + AHEAD < rounds)
        def _():
            send_own(s + AHEAD)

        @pl.when(s < rounds)
        def _():
            forward(s)

        @pl.when((s >= 1) & (s < rounds + 1))
        def _():
            forward_far(s - 1)

        c = s - LAG

        @pl.when(c >= 0)
        def _():
            wait(several(5), near_sem.at[c])
            wait(several(3), far_sem.at[c])
            half = c % HALVES
            u = c // HALVES
            project_keys(c)

            @pl.when(half == HALVES - 1)
            def _():
                finish_keys(u)

            @pl.when(c == per_block)
            def _():
                project_queries(0)

            @pl.when(c == per_block + 1)
            def _():
                reduce_finish(0)

            @pl.when(c == per_block + 3)
            def _():
                gather_finish(0)
                turn(1)

            first = jnp.where(c == per_block + 3, per, u)
            ready = (half == HALVES - 1) & (c != per_block + 1)
            lax.fori_loop(first, jnp.where(ready, u + 1, first), key_step, 0)

            @pl.when(c == per_block - 1)
            def _():
                reduce_send(0)

        return carry

    lax.fori_loop(0, rounds + LAG, step, 0)
    reduce_send(1)
    project_queries(1)
    query_pass(0)

    def drain(s, carry):
        wait(several(15), send_sem.at[s])
        return carry

    lax.fori_loop(0, rounds, drain, 0)
    wait(fast.at[1, 0 : 7 * shard], ag_send_sem.at[0])
    reduce_finish(1)
    gather_finish(1)
    query_pass(1)
    wait(fast.at[2, 0 : 7 * shard], ag_send_sem.at[1])


def local(codes, scales, w_qkv, w_rate, rate_bias, fast_gate, fast_lift, fast_down, out_gain):
    blocks, rows, depth = codes.shape
    head = fast_gate.shape[1]
    sources = lax.axis_size("tensor")
    shards = lax.axis_size("tokens")
    units = blocks * rows // UNIT
    rounds = units * HALVES
    tokens = sources * UNIT
    width = depth // HALVES
    factor = rate_base / math.sqrt(rows * sources * shards)
    stacked = 3 * head + PAD
    columns = w_qkv.shape[1] + w_rate.shape[1]
    vmem = pl.BlockSpec(memory_space=pltpu.VMEM)
    smem = pl.BlockSpec(memory_space=pltpu.SMEM)
    anyspace = pl.BlockSpec(memory_space=pl.ANY)
    dma = pltpu.SemaphoreType.DMA
    out = pl.pallas_call(
        functools.partial(kernel, factor),
        out_shape=jax.ShapeDtypeStruct((blocks, head, sources * rows), BF),
        in_specs=[anyspace, vmem, anyspace, anyspace, smem, vmem, vmem, vmem, vmem],
        out_specs=vmem,
        scratch_shapes=[
            pltpu.VMEM((blocks, HALVES, sources, rows, width), BF),
            pltpu.VMEM((columns, depth), BF),
            pltpu.VMEM((blocks * rows, depth), jnp.int32),
            pltpu.VMEM((scales.shape[2], depth), BF),
            pltpu.VMEM((blocks * rows, depth), F32),
            pltpu.VMEM((columns - head, tokens), F32),
            pltpu.VMEM((head, sources * rows), F32),
            pltpu.VMEM((stacked, KEYS), F32),
            pltpu.VMEM((stacked // shards, KEYS), F32),
            pltpu.VMEM((stacked, KEYS), BF),
            pltpu.VMEM((2, shards, stacked // shards, KEYS), BF),
            pltpu.VMEM((3, stacked, KEYS), BF),
            pltpu.VMEM((2, 2 * head, head), BF),
            pltpu.VMEM((head, 128), F32),
            pltpu.VMEM((blocks, sources * rows, head), BF),
            pltpu.VMEM((units, head, tokens), BF),
            pltpu.VMEM((units, head, tokens), BF),
            pltpu.VMEM((units, 8, tokens), F32),
            dma((3,)),
            dma((rounds,)),
            dma((rounds,)),
            dma((rounds,)),
            dma((rounds,)),
            dma((rounds,)),
            dma((rounds,)),
            dma((rounds,)),
            dma((2,)),
            dma((2,)),
            dma((2,)),
            dma((2,)),
        ],
        compiler_params=pltpu.CompilerParams(
            collective_id=0, has_side_effects=True, vmem_limit_bytes=58 << 20
        ),
        name="fast_weights",
    )(
        codes.reshape(blocks * rows, depth),
        scales.reshape(blocks * rows, scales.shape[2]),
        w_qkv.T,
        w_rate.T,
        rate_bias.reshape(1, 3),
        fast_gate,
        fast_lift,
        fast_down,
        out_gain,
    )
    return jnp.transpose(out, (0, 2, 1))


def solution(mesh):
    return jax.shard_map(
        local,
        mesh=mesh,
        in_specs=(
            P(None, ("tokens", "tensor"), None),
            P(None, ("tokens", "tensor"), None),
            P(None, "tensor"),
            P(),
            P("tensor"),
            P("tensor", None, None),
            P("tensor", None, None),
            P("tensor", None, None),
            P("tensor"),
        ),
        out_specs=P(None, "tokens", "tensor"),
        check_vma=False,
    )
```

time: 146 us -> 124 us (0.85)
  local copies, waits for them, and re-layouts: 20.1 us -> 2.21 us
  Pallas kernels: 124 us -> 121 us
    unnamed x2 -> x1, local copies, waits for them, and re-layouts: 16.6 us -> 2.21 us
    reshape x2 -> x0, local copies, waits for them, and re-layouts: 3.55 us -> none  [the longest x1 2.31 us: local(): return out.reshape(blocks, sources * rows, head)]
    pallas_call x1, Pallas kernels: 124 us -> 121 us  [local(): pl.pallas_call(functools.partial(kernel, factor), out_shape=jax.ShapeDtyp...]
where the time goes in v2:
time: 124 us; the launch traced here: 123 us
  Pallas kernels  121 us (98%)
  local copies, waits for them, and re-layouts  2.21 us (2%)
    pallas_call x1, Pallas kernels, local(): pl.pallas_call(functools.partial(kernel, factor), out_shape=jax.ShapeDtyp...  121 us

profile of v2, /device:TPU:0, one launch (start us, length us, event | category | flops | bytes accessed | tf_op | source)
XLA Modules:
  0.0 123.1 jit_solution(2323483452496157805)
XLA Ops:
  0.0 120.9 %fast_weights.1 = bf16[2,320,768]{2,1,0:T(8,128)(2,1)} custom-call(s32[96,5120]{1,0:T(8,128)} %bitcast.8, s32[96,160]{1,0:T(8,128)} %bitcast.10, bf16[960,5120]{1,0:T(8,128)(2,1)} %bitcast.6, bf16[48,5120]{1,0:T(8,128)(2,1)} %bitcast.9, f32[1,3]{1,0:T(1,128)} %bitcast.11, f32[1,320,320]{2,1,0:T(8,128)} %gate_ref.1, f32[1,320,320]{2,1,0:T(8,128)} %lift_ref.1, ...), custom_call_target="tpu_custom_call" | custom-call | tf_op jit(solution)/shard_map/fast_weights/pallas_call | solution.py:445
  120.9 2.2 %copy.11 = bf16[2,768,320]{1,2,0:T(8,128)(2,1)} copy(bf16[2,768,320]{1,2,0:T(8,128)(2,1)} %bitcast.7) | data formatting | bytes 1966080

commit v3 on v2

--- a/solution.py
+++ b/solution.py
@@ -18,7 +18,7 @@
 UNIT = 16
 HALVES = 2
 AHEAD = 1
-LAG = 2
+LAG = 3
 KEYS = 384
 PAD = 64
 
@@ -61,6 +61,7 @@
     fast,
     gate_lift,
     gains,
+    made,
     queries,
     keys,
     values,
@@ -68,11 +69,15 @@
     local_sem,
     send_sem,
     z_sem,
+    z2_sem,
     x_sem,
-    part_a_sem,
-    part_b_sem,
+    a_sem,
+    a2_sem,
+    b_sem,
+    b2_sem,
     near_sem,
-    far_sem,
+    q_send_sem,
+    q_sem,
     rs_send_sem,
     rs_sem,
     ag_send_sem,
@@ -82,7 +87,9 @@
     per = rows_dev // UNIT
     units = blocks * per
     rounds = units * HALVES
-    part_a = width * 2 // 5 // 128 * 128
+    part_a = width * 5 // 9 // 128 * 128
+    middle = width // 256 * 128
+    middle_a = part_a // 256 * 128
     depth = w.shape[1]
     head = gate_ref.shape[1]
     tokens = sources * UNIT
@@ -97,15 +104,16 @@
         side = 1 - hi if other else hi
         return lax.rem(z + dz, 4) * 4 + side * 2 + core
 
-    z_peers = [at(dz, False) for dz in (1, 3, 2)]
-    x_peer = at(0, True)
-    diagonal = [at(dz, True) for dz in (1, 3, 2)]
+    up, down, across = at(1, False), at(3, False), at(2, False)
+    x_peer, t_other = at(0, True), lax.rem(t + 4, shards)
+    far_up, far_down, far_across = at(1, True), at(3, True), at(2, True)
     sibling = h + 1 - 2 * core
     t_peers = [lax.rem(t + k, shards) for k in range(1, shards)]
 
     barrier = pltpu.get_barrier_semaphore()
-    for peer in z_peers + [x_peer, sibling]:
+    for peer in (up, down, sibling):
         pl.semaphore_signal(barrier, inc=1, device_id=(t, peer), device_id_type=MESH)
+    pl.semaphore_signal(barrier, inc=1, device_id=(t_other, x_peer), device_id_type=MESH)
     for peer in t_peers:
         pl.semaphore_signal(barrier, inc=1, device_id=(peer, h), device_id_type=MESH)
 
@@ -180,37 +188,50 @@
     def several(n, first=0, last=width):
         return acts.at[0, 0, 0:n, 0:UNIT, first:last]
 
+    def move(s, source, first, last, sem, ten, tok=t):
+        part = item(s, source)
+        if last - first < width:
+            part = part.at[:, first:last]
+        remote(part, part, send_sem.at[s], sem.at[s], tok, ten)
+
+    def share(s, source):
+        move(s, source, 0, width, near_sem, sibling)
+
     def send_own(s):
-        mine = item(s, h)
-        for peer in z_peers:
-            remote(mine, mine, send_sem.at[s], z_sem.at[s], t, peer)
-        remote(mine, mine, send_sem.at[s], x_sem.at[s], t, x_peer)
-        remote(mine, mine, send_sem.at[s], near_sem.at[s], t, sibling)
+        move(s, h, 0, width, z_sem, up)
+        move(s, h, 0, width, z_sem, down)
+        move(s, h, 0, width, x_sem, x_peer, t_other)
+        share(s, h)
 
     def forward(s):
-        wait(several(3), z_sem.at[s])
-        for peer in z_peers:
-            part = item(s, peer).at[:, part_a:width]
-            remote(part, part, send_sem.at[s], part_b_sem.at[s], t, x_peer)
-        for peer in z_peers:
-            whole = item(s, peer)
-            remote(whole, whole, send_sem.at[s], near_sem.at[s], t, sibling)
+        wait(several(2), z_sem.at[s])
+        move(s, down, 0, middle, z2_sem, up)
+        move(s, up, middle, width, z2_sem, down)
+        move(s, up, part_a, width, b_sem, x_peer, t_other)
+        move(s, down, part_a, width, b_sem, x_peer, t_other)
         wait(several(1), x_sem.at[s])
-        part = item(s, x_peer).at[:, 0:part_a]
-        for peer in z_peers:
-            remote(part, part, send_sem.at[s], part_a_sem.at[s], t, peer)
-        whole = item(s, x_peer)
-        remote(whole, whole, send_sem.at[s], near_sem.at[s], t, sibling)
-
-    def forward_far(s):
-        wait(several(3, 0, part_a), part_a_sem.at[s])
-        wait(several(3, part_a, width), part_b_sem.at[s])
-        for peer in diagonal:
-            whole = item(s, peer)
-            remote(whole, whole, send_sem.at[s], far_sem.at[s], t, sibling)
+        move(s, x_peer, 0, part_a, a_sem, up)
+        move(s, x_peer, 0, part_a, a_sem, down)
+        for source in (up, down, x_peer):
+            share(s, source)
+
+    def forward_second(s):
+        wait(several(1), z2_sem.at[s])
+        move(s, across, part_a, width, b2_sem, x_peer, t_other)
+        wait(several(2, 0, part_a), a_sem.at[s])
+        move(s, far_down, 0, middle_a, a2_sem, up)
+        move(s, far_up, middle_a, part_a, a2_sem, down)
+        wait(several(2, part_a, width), b_sem.at[s])
+        for source in (across, far_up, far_down):
+            share(s, source)
+
+    def forward_third(s):
+        wait(several(1, 0, part_a), a2_sem.at[s])
+        wait(several(1, part_a, width), b2_sem.at[s])
+        share(s, far_across)
 
     decode(0, 0)
-    pl.semaphore_wait(barrier, 12)
+    pl.semaphore_wait(barrier, 11)
     for s in range(AHEAD):
         if s > 0:
             decode(s, 0)
@@ -252,24 +273,45 @@
 
         lax.fori_loop(0, width // chunk, one, 0)
 
-    def project_queries(block):
+    def project_queries(c):
+        block, half, rows = place(c)
+
         def one(k, carry):
-            half = k // (width // chunk)
-            start = (k % (width // chunk)) * chunk
-            cols = pl.ds(pl.multiple_of(start, chunk), chunk)
-            deep = pl.ds(pl.multiple_of(k * chunk, chunk), chunk)
-            x = acts[block, half, :, :, cols].reshape(block_tokens, chunk)
+            cols = pl.ds(pl.multiple_of(k * chunk, chunk), chunk)
+            deep = pl.ds(pl.multiple_of(half * width + k * chunk, chunk), chunk)
+            x = acts[block, half, :, rows, cols].reshape(tokens, chunk)
             q_acc[...] += dot_nt(w[0:head, deep], x)
             return carry
 
-        q_acc[...] = jnp.zeros_like(q_acc)
-        lax.fori_loop(0, depth // chunk, one, 0)
-        for n in range(block_tokens // 256):
-            q = q_acc[:, n * 256 : (n + 1) * 256]
-            q = q * lax.rsqrt(
-                jnp.sum(q * q, axis=0, keepdims=True) * (1.0 / head) + epsilon
+        @pl.when(half == 0)
+        def _():
+            q_acc[...] = jnp.zeros_like(q_acc)
+
+        lax.fori_loop(0, width // chunk, one, 0)
+
+    def finish_queries(u):
+        block = u // per
+        rows = pl.ds(pl.multiple_of((u % per) * UNIT, UNIT), UNIT)
+        q = q_acc[...]
+        q = q * lax.rsqrt(jnp.sum(q * q, axis=0, keepdims=True) * (1.0 / head) + epsilon)
+        made[block, :, rows, 0:head] = q.T.astype(BF).reshape(sources, UNIT, head)
+        for k in range(4):
+            theirs = pl.ds(k * 4 + (1 - hi) * 2, 2)
+            remote(
+                made.at[block, theirs, rows],
+                queries.at[block, theirs, rows],
+                q_send_sem.at[u],
+                q_sem.at[u],
+                t_other,
+                h,
             )
-            queries[block, n * 256 : (n + 1) * 256] = q.T.astype(BF)
+            mine = pl.ds(k * 4 + hi * 2, 2)
+            queries[block, mine, rows] = made[block, mine, rows]
+
+    def wait_queries(u):
+        sample = queries.at[0, 0:8, 0:UNIT]
+        wait(sample, q_sem.at[u])
+        wait(sample, q_send_sem.at[u])
 
     def finish_keys(u):
         k = kv_acc[0:head]
@@ -345,9 +387,12 @@
         version = block + 1
         down = flip(fast[version, 2 * head : 3 * head, 0:head])
         gain = jnp.concatenate([gains[...], gains[...]], axis=1)
+        for j in range(per):
+            wait_queries(block * per + j)
+        flat = queries[block].reshape(block_tokens, KEYS)
         for n in range(block_tokens // 256):
             span = slice(n * 256, (n + 1) * 256)
-            q = queries[block, span]
+            q = flat[span, 0:head]
             gate_pre = dot(q, fast[version, 0:head, 0:head])
             lift_pre = dot(q, fast[version, head : 2 * head, 0:head])
             hidden = (gate_pre * jax.nn.sigmoid(gate_pre) * lift_pre).astype(BF)
@@ -370,14 +415,17 @@
 
         @pl.when((s >= 1) & (s < rounds + 1))
         def _():
-            forward_far(s - 1)
+            forward_second(s - 1)
+
+        @pl.when((s >= 2) & (s < rounds + 2))
+        def _():
+            forward_third(s - 2)
 
         c = s - LAG
 
         @pl.when(c >= 0)
         def _():
-            wait(several(5), near_sem.at[c])
-            wait(several(3), far_sem.at[c])
+            wait(several(8), near_sem.at[c])
             half = c % HALVES
             u = c // HALVES
             project_keys(c)
@@ -385,10 +433,6 @@
             @pl.when(half == HALVES - 1)
             def _():
                 finish_keys(u)
-
-            @pl.when(c == per_block)
-            def _():
-                project_queries(0)
 
             @pl.when(c == per_block + 1)
             def _():
@@ -407,11 +451,21 @@
             def _():
                 reduce_send(0)
 
+            @pl.when(c < rounds - HALVES)
+            def _():
+                project_queries(c)
+
+                @pl.when(half == HALVES - 1)
+                def _():
+                    finish_queries(u)
+
         return carry
 
     lax.fori_loop(0, rounds + LAG, step, 0)
     reduce_send(1)
-    project_queries(1)
+    for half in range(HALVES):
+        project_queries(rounds - HALVES + half)
+    finish_queries(units - 1)
     query_pass(0)
 
     def drain(s, carry):
@@ -454,7 +508,7 @@
             pltpu.VMEM((scales.shape[2], depth), BF),
             pltpu.VMEM((blocks * rows, depth), F32),
             pltpu.VMEM((columns - head, tokens), F32),
-            pltpu.VMEM((head, sources * rows), F32),
+            pltpu.VMEM((head, tokens), F32),
             pltpu.VMEM((stacked, KEYS), F32),
             pltpu.VMEM((stacked // shards, KEYS), F32),
             pltpu.VMEM((stacked, KEYS), BF),
@@ -462,7 +516,8 @@
             pltpu.VMEM((3, stacked, KEYS), BF),
             pltpu.VMEM((2, 2 * head, head), BF),
             pltpu.VMEM((head, 128), F32),
-            pltpu.VMEM((blocks, sources * rows, head), BF),
+            pltpu.VMEM((blocks, sources, rows, KEYS), BF),
+            pltpu.VMEM((blocks, sources, rows, KEYS), BF),
             pltpu.VMEM((units, head, tokens), BF),
             pltpu.VMEM((units, head, tokens), BF),
             pltpu.VMEM((units, 8, tokens), F32),
@@ -474,6 +529,10 @@
             dma((rounds,)),
             dma((rounds,)),
             dma((rounds,)),
+            dma((rounds,)),
+            dma((rounds,)),
+            dma((units,)),
+            dma((units,)),
             dma((2,)),
             dma((2,)),
             dma((2,)),

time: 124 us -> 107 us (0.86)
  Pallas kernels: 121 us -> 104 us
    pallas_call x1, Pallas kernels: 121 us -> 104 us  [local(): pl.pallas_call(functools.partial(kernel, factor), out_shape=jax.ShapeDtyp...]
where the time goes in v3:
time: 107 us; the launch traced here: 106 us
  Pallas kernels  104 us (97%)
  local copies, waits for them, and re-layouts  2.21 us (2%)
    pallas_call x1, Pallas kernels, local(): pl.pallas_call(functools.partial(kernel, factor), out_shape=jax.ShapeDtyp...  104 us
    unnamed x1, local copies, waits for them, and re-layouts  2.21 us

profile of v3, /device:TPU:0, one launch (start us, length us, event | category | flops | bytes accessed | tf_op | source)
XLA Modules:
  0.0 106.1 jit_solution(365893314860620914)
XLA Ops:
  0.0 103.8 %fast_weights.1 = bf16[2,320,768]{2,1,0:T(8,128)(2,1)} custom-call(s32[96,5120]{1,0:T(8,128)} %bitcast.8, s32[96,160]{1,0:T(8,128)} %bitcast.10, bf16[960,5120]{1,0:T(8,128)(2,1)} %bitcast.6, bf16[48,5120]{1,0:T(8,128)(2,1)} %bitcast.9, f32[1,3]{1,0:T(1,128)} %bitcast.11, f32[1,320,320]{2,1,0:T(8,128)} %gate_ref.1, f32[1,320,320]{2,1,0:T(8,128)} %lift_ref.1, ...), custom_call_target="tpu_custom_call" | custom-call | tf_op jit(solution)/shard_map/fast_weights/pallas_call | solution.py:499
  103.8 2.2 %copy.11 = bf16[2,768,320]{1,2,0:T(8,128)(2,1)} copy(bf16[2,768,320]{1,2,0:T(8,128)(2,1)} %bitcast.7) | data formatting | bytes 1966080

commit v4 on v3

--- a/solution.py
+++ b/solution.py
@@ -18,8 +18,9 @@
 UNIT = 16
 HALVES = 2
 AHEAD = 1
-LAG = 3
+LAG = 4
 KEYS = 384
+SUB = 64
 PAD = 64
 
 
@@ -58,6 +59,8 @@
     master,
     rs_send,
     rs_recv,
+    gathered,
+    first_weights,
     fast,
     gate_lift,
     gains,
@@ -123,6 +126,12 @@
         wrate_hbm, w.at[3 * head : w.shape[0]], local_sem.at[2]
     )
     codes_copy.start()
+    fast_copies = [
+        pltpu.make_async_copy(ref, first_weights.at[i], local_sem.at[3 + i])
+        for i, ref in enumerate((gate_ref, lift_ref, down_ref))
+    ]
+    for copy in fast_copies:
+        copy.start()
     w_copy.start()
     rate_copy.start()
 
@@ -236,16 +245,15 @@
         if s > 0:
             decode(s, 0)
         send_own(s)
-    lax.fori_loop(AHEAD, rounds, decode, 0)
 
     stack[...] = jnp.zeros_like(stack)
-    stack[0:head, 0:head] = gate_ref[0]
-    stack[head : 2 * head, 0:head] = lift_ref[0]
-    stack[2 * head : 3 * head, 0:head] = down_ref[0]
+    for i, copy in enumerate(fast_copies):
+        copy.wait()
+        stack[i * head : (i + 1) * head, 0:head] = first_weights[i, 0]
     fast[0] = stack[...].astype(BF)
-    shard = stack.shape[0] // shards
-    own_rows = pl.ds(pl.multiple_of(t * shard, shard), shard)
-    master[...] = stack[own_rows, :]
+    for part in range(2):
+        own_rows = pl.ds(pl.multiple_of((part * shards + t) * SUB, SUB), SUB)
+        master[part] = stack[own_rows, 0:head]
     stack[...] = jnp.zeros_like(stack)
     gains[...] = jnp.broadcast_to(gain_ref[...][None, :], (128, head)).T
 
@@ -344,29 +352,47 @@
         stack[2 * head : 3 * head, 0:head] += dot_nt(hidden, v)
         return carry
 
+    def pack(x):
+        third = jnp.concatenate(
+            [x[0 : SUB // 2, 256 : 256 + PAD], x[SUB // 2 : SUB, 256 : 256 + PAD]], axis=1
+        )
+        return jnp.concatenate([x[:, 0:128], x[:, 128:256], third], axis=0).astype(BF)
+
+    def unpack(p):
+        p = p.astype(F32)
+        third = p[2 * SUB : 2 * SUB + SUB // 2]
+        third = jnp.concatenate([third[:, 0:PAD], third[:, PAD : 2 * PAD]], axis=0)
+        return jnp.concatenate([p[0:SUB], p[SUB : 2 * SUB], third], axis=1)
+
     def reduce_send(block):
-        rs_send[...] = stack[...].astype(BF)
-        for peer in t_peers:
-            rows = pl.ds(pl.multiple_of(peer * shard, shard), shard)
-            remote(
-                rs_send.at[rows],
-                rs_recv.at[block, t],
-                rs_send_sem.at[block],
-                rs_sem.at[block],
-                peer,
-                h,
-            )
-        rs_recv[block, t] = rs_send[own_rows, :]
+        for part in range(2):
+
+            def pack_one(j, carry, part=part):
+                rows = pl.ds(pl.multiple_of((part * shards + j) * SUB, SUB), SUB)
+                rs_send[part, j] = pack(stack[rows, :])
+                return carry
+
+            lax.fori_loop(0, shards, pack_one, 0)
+            for peer in t_peers:
+                remote(
+                    rs_send.at[part, peer],
+                    rs_recv.at[block, part, t],
+                    rs_send_sem.at[block, part],
+                    rs_sem.at[block, part],
+                    peer,
+                    h,
+                )
+            rs_recv[block, part, t] = rs_send[part, t]
         stack[...] = jnp.zeros_like(stack)
 
-    def reduce_finish(block):
-        wait(rs_recv.at[block, 0:7], rs_sem.at[block])
-        wait(rs_send.at[0 : 7 * shard], rs_send_sem.at[block])
-        summed = rs_recv[block, 0].astype(F32)
+    def reduce_finish(block, part):
+        wait(rs_recv.at[block, part, 0:7], rs_sem.at[block, part])
+        wait(rs_send.at[part, 0:7], rs_send_sem.at[block, part])
+        summed = rs_recv[block, part, 0].astype(F32)
         for j in range(1, shards):
-            summed = summed + rs_recv[block, j].astype(F32)
-        old = master[...]
-        summed = old + summed
+            summed = summed + rs_recv[block, part, j].astype(F32)
+        old = master[part]
+        summed = old + unpack(summed)
         old_scale = jnp.sqrt(
             jnp.sum(old * old, axis=1, keepdims=True) * (1.0 / head) + epsilon
         )
@@ -374,14 +400,28 @@
             jnp.sum(summed * summed, axis=1, keepdims=True) * (1.0 / head) + epsilon
         )
         new = summed * old_scale * new_scale
-        master[...] = new
-        fast[block + 1, own_rows, :] = new.astype(BF)
-        mine = fast.at[block + 1, own_rows]
+        master[part] = new
+        gathered[block, part, t] = pack(new)
+        mine = gathered.at[block, part, t]
         for peer in t_peers:
-            remote(mine, mine, ag_send_sem.at[block], ag_sem.at[block], peer, h)
+            remote(
+                mine, mine, ag_send_sem.at[block, part], ag_sem.at[block, part], peer, h
+            )
 
     def gather_finish(block):
-        wait(fast.at[block + 1, 0 : 7 * shard], ag_sem.at[block])
+        for part in range(2):
+            wait(gathered.at[block, part, 0:7], ag_sem.at[block, part])
+
+            def unpack_one(j, carry, part=part):
+                rows = pl.ds(pl.multiple_of((part * shards + j) * SUB, SUB), SUB)
+                fast[block + 1, rows, 0:head] = unpack(gathered[block, part, j]).astype(BF)
+                return carry
+
+            lax.fori_loop(0, shards, unpack_one, 0)
+
+    def gather_drain(block):
+        for part in range(2):
+            wait(gathered.at[block, part, 0:7], ag_send_sem.at[block, part])
 
     def query_pass(block):
         version = block + 1
@@ -407,57 +447,59 @@
     def step(s, carry):
         @pl.when(s + AHEAD < rounds)
         def _():
+            decode(s + AHEAD, 0)
             send_own(s + AHEAD)
 
         @pl.when(s < rounds)
         def _():
             forward(s)
 
+        c = s - LAG
+        half = c % HALVES
+        u = c // HALVES
+
+        @pl.when(c >= 0)
+        def _():
+            wait(several(8), near_sem.at[c])
+            project_keys(c)
+
         @pl.when((s >= 1) & (s < rounds + 1))
         def _():
             forward_second(s - 1)
 
-        @pl.when((s >= 2) & (s < rounds + 2))
-        def _():
-            forward_third(s - 2)
-
-        c = s - LAG
-
-        @pl.when(c >= 0)
-        def _():
-            wait(several(8), near_sem.at[c])
-            half = c % HALVES
-            u = c // HALVES
-            project_keys(c)
+        @pl.when((c >= 0) & (c < rounds - HALVES))
+        def _():
+            project_queries(c)
 
             @pl.when(half == HALVES - 1)
             def _():
-                finish_keys(u)
-
-            @pl.when(c == per_block + 1)
-            def _():
-                reduce_finish(0)
-
-            @pl.when(c == per_block + 3)
-            def _():
-                gather_finish(0)
-                turn(1)
-
-            first = jnp.where(c == per_block + 3, per, u)
-            ready = (half == HALVES - 1) & (c != per_block + 1)
-            lax.fori_loop(first, jnp.where(ready, u + 1, first), key_step, 0)
-
-            @pl.when(c == per_block - 1)
-            def _():
-                reduce_send(0)
-
-            @pl.when(c < rounds - HALVES)
-            def _():
-                project_queries(c)
-
-                @pl.when(half == HALVES - 1)
-                def _():
-                    finish_queries(u)
+                finish_queries(u)
+
+        @pl.when((c >= 0) & (half == HALVES - 1))
+        def _():
+            finish_keys(u)
+
+        @pl.when((s >= 2) & (s < rounds + 2))
+        def _():
+            forward_third(s - 2)
+
+        @pl.when(c == per_block + 1)
+        def _():
+            reduce_finish(0, 0)
+            reduce_finish(0, 1)
+
+        @pl.when(c == per_block + 3)
+        def _():
+            gather_finish(0)
+            turn(1)
+
+        first = jnp.where(c == per_block + 3, per, u)
+        ready = (c >= 0) & (half == HALVES - 1) & (c != per_block + 1)
+        lax.fori_loop(first, jnp.where(ready, u + 1, first), key_step, 0)
+
+        @pl.when(c == per_block - 1)
+        def _():
+            reduce_send(0)
 
         return carry
 
@@ -466,6 +508,9 @@
     for half in range(HALVES):
         project_queries(rounds - HALVES + half)
     finish_queries(units - 1)
+    gather_drain(0)
+    reduce_finish(1, 0)
+    reduce_finish(1, 1)
     query_pass(0)
 
     def drain(s, carry):
@@ -473,11 +518,9 @@
         return carry
 
     lax.fori_loop(0, rounds, drain, 0)
-    wait(fast.at[1, 0 : 7 * shard], ag_send_sem.at[0])
-    reduce_finish(1)
     gather_finish(1)
     query_pass(1)
-    wait(fast.at[2, 0 : 7 * shard], ag_send_sem.at[1])
+    gather_drain(1)
 
 
 def local(codes, scales, w_qkv, w_rate, rate_bias, fast_gate, fast_lift, fast_down, out_gain):
@@ -499,7 +542,7 @@
     out = pl.pallas_call(
         functools.partial(kernel, factor),
         out_shape=jax.ShapeDtypeStruct((blocks, head, sources * rows), BF),
-        in_specs=[anyspace, vmem, anyspace, anyspace, smem, vmem, vmem, vmem, vmem],
+        in_specs=[anyspace, vmem, anyspace, anyspace, smem] + [anyspace] * 3 + [vmem],
         out_specs=vmem,
         scratch_shapes=[
             pltpu.VMEM((blocks, HALVES, sources, rows, width), BF),
@@ -510,9 +553,11 @@
             pltpu.VMEM((columns - head, tokens), F32),
             pltpu.VMEM((head, tokens), F32),
             pltpu.VMEM((stacked, KEYS), F32),
-            pltpu.VMEM((stacked // shards, KEYS), F32),
-            pltpu.VMEM((stacked, KEYS), BF),
-            pltpu.VMEM((2, shards, stacked // shards, KEYS), BF),
+            pltpu.VMEM((2, SUB, head), F32),
+            pltpu.VMEM((2, shards, SUB * 5 // 2, 128), BF),
+            pltpu.VMEM((2, 2, shards, SUB * 5 // 2, 128), BF),
+            pltpu.VMEM((2, 2, shards, SUB * 5 // 2, 128), BF),
+            pltpu.VMEM((3, 1, head, head), F32),
             pltpu.VMEM((3, stacked, KEYS), BF),
             pltpu.VMEM((2, 2 * head, head), BF),
             pltpu.VMEM((head, 128), F32),
@@ -521,7 +566,7 @@
             pltpu.VMEM((units, head, tokens), BF),
             pltpu.VMEM((units, head, tokens), BF),
             pltpu.VMEM((units, 8, tokens), F32),
-            dma((3,)),
+            dma((6,)),
             dma((rounds,)),
             dma((rounds,)),
             dma((rounds,)),
@@ -533,10 +578,10 @@
             dma((rounds,)),
             dma((units,)),
             dma((units,)),
-            dma((2,)),
-            dma((2,)),
-            dma((2,)),
-            dma((2,)),
+            dma((2, 2)),
+            dma((2, 2)),
+            dma((2, 2)),
+            dma((2, 2)),
         ],
         compiler_params=pltpu.CompilerParams(
             collective_id=0, has_side_effects=True, vmem_limit_bytes=58 << 20

time: 107 us -> 100 us (0.935)
  Pallas kernels: 104 us -> 97.7 us
    pallas_call x1, Pallas kernels: 104 us -> 97.7 us  [local(): pl.pallas_call(functools.partial(kernel, factor), out_shape=jax.ShapeDtyp...]
where the time goes in v4:
time: 100 us; the launch traced here: 99.9 us
  Pallas kernels  97.7 us (98%)
  local copies, waits for them, and re-layouts  2.21 us (2%)
    pallas_call x1, Pallas kernels, local(): pl.pallas_call(functools.partial(kernel, factor), out_shape=jax.ShapeDtyp...  97.7 us
    unnamed x1, local copies, waits for them, and re-layouts  2.21 us

profile of v4, /device:TPU:0, one launch (start us, length us, event | category | flops | bytes accessed | tf_op | source)
XLA Modules:
  0.0 99.9 jit_solution(10629067724430857248)
XLA Ops:
  0.0 97.7 %fast_weights.1 = bf16[2,320,768]{2,1,0:T(8,128)(2,1)} custom-call(s32[96,5120]{1,0:T(8,128)} %bitcast.8, s32[96,160]{1,0:T(8,128)} %bitcast.10, bf16[960,5120]{1,0:T(8,128)(2,1)} %bitcast.6, bf16[48,5120]{1,0:T(8,128)(2,1)} %bitcast.9, f32[1,3]{1,0:T(1,128)} %bitcast.11, f32[1,320,320]{2,1,0:T(8,128)} %gate_ref.1, f32[1,320,320]{2,1,0:T(8,128)} %lift_ref.1, ...), custom_call_target="tpu_custom_call" | custom-call | tf_op jit(solution)/shard_map/fast_weights/pallas_call | solution.py:542
  97.7 2.2 %copy.11 = bf16[2,768,320]{1,2,0:T(8,128)(2,1)} copy(bf16[2,768,320]{1,2,0:T(8,128)(2,1)} %bitcast.7) | data formatting | bytes 1966080

commit v5 on v4

--- a/solution.py
+++ b/solution.py
@@ -18,7 +18,7 @@
 UNIT = 16
 HALVES = 2
 AHEAD = 1
-LAG = 4
+LAG = 3
 KEYS = 384
 SUB = 64
 PAD = 64
@@ -207,9 +207,9 @@
         move(s, source, 0, width, near_sem, sibling)
 
     def send_own(s):
+        move(s, h, 0, width, x_sem, x_peer, t_other)
         move(s, h, 0, width, z_sem, up)
         move(s, h, 0, width, z_sem, down)
-        move(s, h, 0, width, x_sem, x_peer, t_other)
         share(s, h)
 
     def forward(s):
@@ -486,16 +486,21 @@
         @pl.when(c == per_block + 1)
         def _():
             reduce_finish(0, 0)
+
+        @pl.when(c == per_block + 2)
+        def _():
             reduce_finish(0, 1)
 
-        @pl.when(c == per_block + 3)
+        @pl.when(c == per_block + 4)
         def _():
             gather_finish(0)
             turn(1)
 
-        first = jnp.where(c == per_block + 3, per, u)
-        ready = (c >= 0) & (half == HALVES - 1) & (c != per_block + 1)
-        lax.fori_loop(first, jnp.where(ready, u + 1, first), key_step, 0)
+        begin = per_block + 4
+        usual = (c >= 0) & (half == HALVES - 1) & ((c < per_block) | (c > begin))
+        first = jnp.where(c == begin, per, u)
+        last = jnp.where(c == begin, (begin + 1) // HALVES, jnp.where(usual, u + 1, u))
+        lax.fori_loop(first, last, key_step, 0)
 
         @pl.when(c == per_block - 1)
         def _():

time: 100 us -> 98 us (0.980)
  Pallas kernels: 97.7 us -> 95.6 us
    pallas_call x1, Pallas kernels: 97.7 us -> 95.6 us  [local(): pl.pallas_call(functools.partial(kernel, factor), out_shape=jax.ShapeDtyp...]
where the time goes in v5:
time: 98 us; the launch traced here: 97.8 us
  Pallas kernels  95.6 us (98%)
  local copies, waits for them, and re-layouts  2.21 us (2%)
    pallas_call x1, Pallas kernels, local(): pl.pallas_call(functools.partial(kernel, factor), out_shape=jax.ShapeDtyp...  95.6 us
    unnamed x1, local copies, waits for them, and re-layouts  2.21 us

profile of v5, /device:TPU:0, one launch (start us, length us, event | category | flops | bytes accessed | tf_op | source)
XLA Modules:
  0.0 97.8 jit_solution(16466808087913141958)
XLA Ops:
  0.0 95.6 %fast_weights.1 = bf16[2,320,768]{2,1,0:T(8,128)(2,1)} custom-call(s32[96,5120]{1,0:T(8,128)} %bitcast.8, s32[96,160]{1,0:T(8,128)} %bitcast.10, bf16[960,5120]{1,0:T(8,128)(2,1)} %bitcast.6, bf16[48,5120]{1,0:T(8,128)(2,1)} %bitcast.9, f32[1,3]{1,0:T(1,128)} %bitcast.11, f32[1,320,320]{2,1,0:T(8,128)} %gate_ref.1, f32[1,320,320]{2,1,0:T(8,128)} %lift_ref.1, ...), custom_call_target="tpu_custom_call" | custom-call | tf_op jit(solution)/shard_map/fast_weights/pallas_call | solution.py:547
  95.6 2.2 %copy.11 = bf16[2,768,320]{1,2,0:T(8,128)(2,1)} copy(bf16[2,768,320]{1,2,0:T(8,128)(2,1)} %bitcast.7) | data formatting | bytes 1966080

commit v6 on v5

--- a/solution.py
+++ b/solution.py
@@ -450,10 +450,6 @@
             decode(s + AHEAD, 0)
             send_own(s + AHEAD)
 
-        @pl.when(s < rounds)
-        def _():
-            forward(s)
-
         c = s - LAG
         half = c % HALVES
         u = c // HALVES
@@ -463,9 +459,9 @@
             wait(several(8), near_sem.at[c])
             project_keys(c)
 
-        @pl.when((s >= 1) & (s < rounds + 1))
-        def _():
-            forward_second(s - 1)
+        @pl.when(s < rounds)
+        def _():
+            forward(s)
 
         @pl.when((c >= 0) & (c < rounds - HALVES))
         def _():
@@ -474,6 +470,10 @@
             @pl.when(half == HALVES - 1)
             def _():
                 finish_queries(u)
+
+        @pl.when((s >= 1) & (s < rounds + 1))
+        def _():
+            forward_second(s - 1)
 
         @pl.when((c >= 0) & (half == HALVES - 1))
         def _():

time: 98 us -> 97.1 us (level)
  Pallas kernels: 95.6 us -> 94.6 us
    pallas_call x1, Pallas kernels: 95.6 us -> 94.6 us  [local(): pl.pallas_call(functools.partial(kernel, factor), out_shape=jax.ShapeDtyp...]
where the time goes in v6:
time: 97.1 us; the launch traced here: 96.8 us
  Pallas kernels  94.6 us (97%)
  local copies, waits for them, and re-layouts  2.21 us (2%)
    pallas_call x1, Pallas kernels, local(): pl.pallas_call(functools.partial(kernel, factor), out_shape=jax.ShapeDtyp...  94.6 us
    unnamed x1, local copies, waits for them, and re-layouts  2.21 us

profile of v6, /device:TPU:0, one launch (start us, length us, event | category | flops | bytes accessed | tf_op | source)
XLA Modules:
  0.0 96.8 jit_solution(18320897806644628195)
XLA Ops:
  0.0 94.6 %fast_weights.1 = bf16[2,320,768]{2,1,0:T(8,128)(2,1)} custom-call(s32[96,5120]{1,0:T(8,128)} %bitcast.8, s32[96,160]{1,0:T(8,128)} %bitcast.10, bf16[960,5120]{1,0:T(8,128)(2,1)} %bitcast.6, bf16[48,5120]{1,0:T(8,128)(2,1)} %bitcast.9, f32[1,3]{1,0:T(1,128)} %bitcast.11, f32[1,320,320]{2,1,0:T(8,128)} %gate_ref.1, f32[1,320,320]{2,1,0:T(8,128)} %lift_ref.1, ...), custom_call_target="tpu_custom_call" | custom-call | tf_op jit(solution)/shard_map/fast_weights/pallas_call | solution.py:547
  94.6 2.2 %copy.11 = bf16[2,768,320]{1,2,0:T(8,128)(2,1)} copy(bf16[2,768,320]{1,2,0:T(8,128)(2,1)} %bitcast.7) | data formatting | bytes 1966080
